TPU v7x, 256 devices: a whole 4x4x8 slice. The times are simulated.
256 devices in a mesh: comp: 8 (over x, core), tx: 8 (over z), ty: 4 (over y).
Axes of the slice: x: 4, y: 4, z: 8, core: 2. Of those that a mesh axis runs over, the one named last changes fastest.
Arguments:
- spectrum: float32 [1800, 64, 1024], P('comp', 'tx', 'ty'), may hold values from 0.05 to 2
- sea_mask: int32 [64, 1024], P('tx', 'ty'), may hold values from 0 to 1, as said below
- owner_list: int32 [8, 4, 64, 32], P('tx', 'ty'), may hold values from 0 to 2047, as said below
- owner_count: int32 [8, 4, 64], P('tx', 'ty'), may hold values from 0 to 32, as said below
- slopes: float32 [2, 64, 1024], P(None, 'tx', 'ty'), may hold values from -0.00015 to 0.00015
- friction: float32 [64, 1024], P('tx', 'ty'), may hold values from 0.15 to 0.6
- wind_angle: float32 [64, 1024], P('tx', 'ty'), may hold values from -3.140625 to 3.140625
Outputs:
- new_spectrum: float32 [1800, 64, 1024], P('comp', 'tx', 'ty')
Inputs may be any that keep to these rules, and one draw needn't show every extreme that they name: `sea_mask`: 1 marks sea, 0 land. Each row of tiles along tx holds a tile without land, and each latitude row of a tile has a sea cell. `owner_list`: owner o is the device of index o along comp+tx (comp slowest) in the same row of tiles. For each tile, the first owner_count slots of each owner name cells of the tile as ix * 256 + iy; together they name every sea cell of the tile exactly once and no land cell. The other slots hold 0. `owner_count`: points of one tile given to one owner, at most 32; 32 is reached in every draw.
All inputs are finite; a program needn't handle non-finite values.
Results may differ from a plain program's by a relative error of at most 0.0003.
Values sent between devices are 32-bit elements; how exact they have to be, the bound alone decides.
A program may use at most 64 MiB of HBM per device.

v0:
```python
import math

import jax
import jax.numpy as jnp
import numpy as np
from jax import lax
from jax.experimental import pallas as pl
from jax.experimental.pallas import tpu as pltpu
from jax.sharding import PartitionSpec as P

NDIR = 36
NFREQ = 50
HALF = 25
OWN = 9
REACH = 16
ROWS = 8
COLS = 256
TALL = HALF * ROWS
PACK = 32

TIME_STEP = 240.0
CELL_SIZE = 11100.0
GRAVITY = 9.81
LOW_FREQ = 0.0373
HIGH_FREQ = 1.0
WIND_GROWTH = 0.0001
WIND_FACTOR = 28.0
SATURATION_LOSS = 0.0005
CUMULATIVE_LOSS = 0.001
STEEPNESS_LOSS = 0.005
SATURATION_LEVEL = 0.6

T_COS, T_SIN, T_SPEED, T_BEND, T_OMEGA, T_STEEP = 0, 36, 72, 122, 172, 222


def tables():
    heading = 2.0 * math.pi / NDIR * np.arange(NDIR)
    omega = 2.0 * math.pi * LOW_FREQ * (HIGH_FREQ / LOW_FREQ) ** (np.arange(NFREQ) / (NFREQ - 1))
    speed = TIME_STEP / CELL_SIZE * GRAVITY / (2.0 * omega)
    bend = TIME_STEP * NDIR / (2.0 * math.pi) * (2.0 * math.pi * LOW_FREQ) / omega
    steep = (omega / omega[-1]) ** 2 / (NDIR * NFREQ)
    return np.concatenate([np.cos(heading), np.sin(heading), speed, bend, omega, steep]).astype(
        np.float32
    )


def spread_weights():
    weights = np.cos(2.0 * math.pi / NDIR * np.arange(REACH // 2 + 1)) ** 2
    total = weights[0] + 2.0 * np.sum(weights[1:])
    return [float(w) for w in weights / total / SATURATION_LEVEL]


def kernel(
    spec,
    table,
    sea_mask,
    slopes,
    friction,
    wind,
    out,
    raw,
    moved,
    lon_out,
    lon_in,
    lat_out,
    lat_in,
    steep,
    offset,
    own_sem,
    raw_send,
    raw_recv,
    lon_send,
    lon_recv,
    lat_send,
    lat_recv,
    near_send,
    link_send,
    far_send,
    relay_send,
    block_recv,
    steep_send,
    steep_recv,
    offset_send,
    offset_recv,
):
    comp = lax.axis_index("comp")
    tx = lax.axis_index("tx")
    ty = lax.axis_index("ty")
    parity = comp % 2
    quadrant = comp // 2
    pos_x = 1 - ((quadrant + 1) // 2) % 2
    pos_y = 1 - quadrant // 2

    def at_comp(step):
        return {"comp": (comp + step + 8) % 8}

    def remote(src, dst, send, recv, device):
        return pltpu.make_async_remote_copy(
            src_ref=src,
            dst_ref=dst,
            send_sem=send,
            recv_sem=recv,
            device_id=device,
            device_id_type=pl.DeviceIdType.MESH,
        )

    load_own = pltpu.make_async_copy(spec, raw.at[2 : 2 + OWN], own_sem)
    load_own.start()
    barrier = pltpu.get_barrier_semaphore()
    for step in range(1, 8):
        pl.semaphore_signal(
            barrier, inc=1, device_id=at_comp(step), device_id_type=pl.DeviceIdType.MESH
        )
    for step in (1, -1):
        pl.semaphore_signal(
            barrier,
            inc=1,
            device_id={"tx": (tx + step + 8) % 8},
            device_id_type=pl.DeviceIdType.MESH,
        )
        pl.semaphore_signal(
            barrier,
            inc=1,
            device_id={"ty": (ty + step + 4) % 4},
            device_id_type=pl.DeviceIdType.MESH,
        )

    sea = sea_mask[...].astype(jnp.float32)
    row_ids = lax.broadcasted_iota(jnp.int32, (ROWS, COLS), 0)
    lane_ids = lax.broadcasted_iota(jnp.int32, (ROWS, 128), 1)
    inflow_row = jnp.where(row_ids == (1 - pos_x) * (ROWS - 1), 1.0, 0.0) > 0.5
    inflow_lane = jnp.where(lane_ids == (1 - pos_y) * 127, 1.0, 0.0) > 0.5
    up_y = jnp.zeros((ROWS, 128), jnp.int32) + pos_y > 0
    row_shift = jnp.where(pos_x > 0, 1, ROWS - 1)
    lane_shift = jnp.where(pos_y > 0, 1, 127)

    last_row = pos_x * (ROWS - 1)
    last_lane = pos_y * 127
    last_half = pl.multiple_of(pos_y * 128, 128)
    sea_row = jnp.sum(jnp.where(row_ids == last_row, sea, 0.0), axis=0, keepdims=True)
    sea_half = jnp.where(up_y, sea[:, 128:], sea[:, :128])

    load_own.wait()

    def first_block(phase):
        return (phase + parity) % 2

    def pack(phase):
        first = first_block(phase)

        def pack_block(t, carry):
            block = first + 2 * t
            lon_out[phase, t, pl.ds(PACK - ROWS, ROWS), :] = jnp.zeros((ROWS, COLS), jnp.float32)

            def pack_one(j, lat):
                lon_out[phase, t, pl.ds(j, 1), :] = (
                    raw[2 + block, pl.ds(ROWS * j + last_row, 1), :] * sea_row
                )
                side = raw[2 + block, pl.ds(pl.multiple_of(ROWS * j, ROWS), ROWS), pl.ds(last_half, 128)]
                turned = pltpu.roll(side * sea_half, (j - last_lane + 128) % 128, 1)
                return jnp.where(lane_ids == j, turned, lat)

            lat_out[phase, t] = lax.fori_loop(
                0, HALF, pack_one, jnp.zeros((ROWS, 128), jnp.float32), unroll=5
            )
            return carry

        lax.fori_loop(0, 5 - first, pack_block, 0)

    lat_out[...] = jnp.zeros(lat_out.shape, jnp.float32)
    pack(0)
    pl.semaphore_wait(barrier, 11)

    def raw_copies(phase):
        first = first_block(phase)
        return [
            remote(
                raw.at[2 + first],
                raw.at[11 + first],
                raw_send.at[phase, 0],
                raw_recv.at[phase, 0],
                at_comp(-1),
            ),
            remote(
                raw.at[10 - first],
                raw.at[1 - first],
                raw_send.at[phase, 1],
                raw_recv.at[phase, 1],
                at_comp(1),
            ),
        ]

    lon_to = {"tx": (tx + 2 * pos_x - 1 + 8) % 8}
    lat_to = {"ty": (ty + 2 * pos_y - 1 + 4) % 4}

    def lon_copy(phase, start, count, which):
        return remote(
            lon_out.at[phase, start : start + count],
            lon_in.at[phase, start : start + count],
            lon_send.at[phase, which],
            lon_recv.at[phase, which],
            lon_to,
        )

    def lat_copy(phase):
        return remote(
            lat_out.at[phase], lat_in.at[phase], lat_send.at[phase], lat_recv.at[phase], lat_to
        )

    def send_halos(phase):
        for copy in raw_copies(phase):
            copy.start()
        lon_copy(phase, 0, 4, 0).start()

        @pl.when(first_block(phase) == 0)
        def _():
            lon_copy(phase, 4, 1, 1).start()

        lat_copy(phase).start()

    def wait_halos(phase):
        for copy in raw_copies(phase):
            copy.wait_send()
        first = first_block(phase)
        remote(raw.at[2], raw.at[12 - first], raw_send.at[phase, 0], raw_recv.at[phase, 0], at_comp(1)).wait_recv()
        remote(raw.at[2], raw.at[first], raw_send.at[phase, 1], raw_recv.at[phase, 1], at_comp(1)).wait_recv()
        lon_copy(phase, 0, 4, 0).wait()

        @pl.when(first_block(phase) == 0)
        def _():
            lon_copy(phase, 4, 1, 1).wait()

        lat_copy(phase).wait()

    lat_open = jnp.where(pos_y > 0, ty, 3 - ty) > 0
    lat_gate = jnp.where(lat_open, 1.0, 0.0)
    slope_x = slopes[0]
    slope_y = slopes[1]

    def advect(phase, steepness):
        first = first_block(phase)

        def one_block(t, steepness):
            block = first + 2 * t
            place = OWN * comp + block
            heading = place // 2
            freq = HALF * (place % 2)
            cos = table[T_COS + heading]
            sin = table[T_SIN + heading]
            abs_cos = jnp.abs(cos)
            abs_sin = jnp.abs(sin)
            bend_x = sin * slope_x - cos * slope_y
            lat = lat_in[phase, t] * lat_gate

            def one(j, steepness):
                rows = pl.ds(pl.multiple_of(ROWS * j, ROWS), ROWS)
                centre = raw[2 + block, rows, :]
                prev_dir = raw[block, rows, :]
                next_dir = raw[4 + block, rows, :]
                masked = centre * sea
                up_lon = jnp.where(
                    inflow_row,
                    jnp.broadcast_to(lon_in[phase, t, pl.ds(j, 1), :], (ROWS, COLS)),
                    pltpu.roll(masked, row_shift, 0),
                )
                side = pltpu.roll(lat, (last_lane_in - j + 128) % 128, 1)
                low = pltpu.roll(masked[:, :128], lane_shift, 1)
                high = pltpu.roll(masked[:, 128:], lane_shift, 1)
                low_up = jnp.where(inflow_lane, jnp.where(up_y, side, high), low)
                high_up = jnp.where(inflow_lane, jnp.where(up_y, low, side), high)
                up_lat = jnp.concatenate([low_up, high_up], axis=1)
                speed = table[T_SPEED + freq + j]
                turning = table[T_BEND + freq + j] * bend_x
                value = sea * (
                    centre
                    - (speed * abs_cos) * (centre - up_lon)
                    - (speed * abs_sin) * (centre - up_lat)
                    - (
                        jnp.maximum(turning, 0.0) * (centre - prev_dir)
                        + jnp.minimum(turning, 0.0) * (next_dir - centre)
                    )
                )
                moved[REACH + block, rows, :] = value
                return steepness + table[T_STEEP + freq + j] * value

            return lax.fori_loop(0, HALF, one, steepness, unroll=5)

        return lax.fori_loop(0, 5 - first, one_block, steepness)

    last_lane_in = (1 - pos_y) * 127

    def shifted(side, phase, action):
        first = (phase + side) % 2
        mine = list(range(first, OWN, 2))
        far = [b for b in mine if (b >= 2 if side == 0 else b <= 6)]
        theirs = list(range(1 - first, OWN, 2))
        relay = [b for b in theirs if (b >= 2 if side == 0 else b <= 6)]
        link = [b for b in mine if (b <= 6 if side == 0 else b >= 2)]
        link += [b for b in mine if b not in link]
        partner, other = (1, -1) if side == 0 else (-1, 1)

        def block_copy(src, dst, sems, device):
            return remote(moved.at[src], moved.at[dst], sems.at[src], block_recv.at[dst], device)

        def arrived(dst):
            block_copy(REACH, dst, near_send, at_comp(1)).wait_recv()

        links = [
            block_copy(REACH + b, REACH + b - OWN * other, link_send, at_comp(other)) for b in link
        ]
        fars = [
            block_copy(REACH + b, REACH + b - 2 * OWN * partner, far_send, at_comp(2 * partner))
            for b in far
        ]
        nears = [
            block_copy(REACH + b, REACH + b - OWN * partner, near_send, at_comp(partner))
            for b in mine
        ]
        relay_from = [REACH + b + OWN * other for b in relay]
        relays = [
            block_copy(src, src - OWN * partner, relay_send, at_comp(partner)) for src in relay_from
        ]
        if action == "send":
            for copy in links + fars + nears:
                copy.start()
        elif action == "relay":
            for src, copy in zip(relay_from, relays):
                arrived(src)
                copy.start()
        elif action == "receive":
            for b in theirs:
                arrived(REACH + b + OWN * partner)
                if b not in relay:
                    arrived(REACH + b + OWN * other)
            for b in mine:
                if b in far:
                    pass
            far_in = [b for b in mine if (b >= 2 if side == 0 else b <= 6)]
            for b in far_in:
                arrived(REACH + b - 2 * OWN * partner)
            for b in mine:
                if b <= 6 if side == 0 else b >= 2:
                    arrived(REACH + b + 2 * OWN * partner)
        else:
            for copy in links + fars + nears + relays:
                copy.wait_send()

    def exchange(phase, action):
        for side in (0, 1):

            @pl.when(parity == side)
            def _():
                shifted(side, phase, action)

    def steep_copy(step):
        return remote(
            steep.at[comp], steep.at[comp], steep_send.at[step], steep_recv.at[comp], at_comp(step)
        )

    send_halos(0)
    pack(1)
    send_halos(1)
    wait_halos(0)
    partial = advect(0, jnp.zeros((ROWS, COLS), jnp.float32))
    exchange(0, "send")
    wait_halos(1)
    partial = advect(1, partial)
    exchange(1, "send")
    steep[comp] = partial
    for step in range(1, 8):
        steep_copy(step).start()

    weights = spread_weights()
    wind_x = (WIND_FACTOR / GRAVITY) * friction[...] * jnp.cos(wind[...])
    wind_y = (WIND_FACTOR / GRAVITY) * friction[...] * jnp.sin(wind[...])

    for step in range(1, 8):
        slot = (comp + step) % 8
        remote(
            steep.at[slot], steep.at[slot], steep_send.at[step], steep_recv.at[slot], at_comp(step)
        ).wait_recv()
    total = steep[0]
    for slot in range(1, 8):
        total = total + steep[slot]
    steep_loss = (TIME_STEP * STEEPNESS_LOSS) * total * total
    at_sea = sea > 0.5

    def sources(phase):
        first = first_block(phase)

        def one_block(t, carry):
            block = first + 2 * t
            place = OWN * comp + block
            heading = place // 2
            freq = HALF * (place % 2)
            cos = table[T_COS + heading]
            sin = table[T_SIN + heading]
            along = cos * wind_x + sin * wind_y

            def one(j, running):
                rows = pl.ds(pl.multiple_of(ROWS * j, ROWS), ROWS)
                centre = moved[REACH + block, rows, :]
                level = weights[0] * centre
                for m in range(1, REACH // 2 + 1):
                    level = level + weights[m] * (
                        moved[REACH + block - 2 * m, rows, :] + moved[REACH + block + 2 * m, rows, :]
                    )
                excess = jnp.maximum(level - 1.0, 0.0)
                excess_sq = excess * excess
                omega = table[T_OMEGA + freq + j]
                growth = (TIME_STEP * WIND_GROWTH * omega) * jnp.maximum(omega * along - 1.0, 0.0)
                losses = omega * (
                    (TIME_STEP * SATURATION_LOSS) * excess_sq
                    + (TIME_STEP * CUMULATIVE_LOSS / NFREQ) * running
                    + steep_loss
                )
                updated = centre * (1.0 + growth) / (1.0 + losses)
                out[block, rows, :] = jnp.where(at_sea, updated, centre)
                return running + excess_sq

            if phase == 0:
                start = jnp.zeros((ROWS, COLS), jnp.float32)
            else:
                start = offset[block]
            offset[block + 1] = lax.fori_loop(0, HALF, one, start, unroll=5)
            return carry

        lax.fori_loop(0, 5 - first, one_block, 0)

    offset_copy = remote(
        offset.at[OWN], offset.at[0], offset_send, offset_recv, {"comp": comp + 1 - 2 * parity}
    )
    exchange(0, "relay")
    exchange(0, "receive")
    sources(0)

    @pl.when(parity == 0)
    def _():
        offset_copy.start()

    exchange(1, "relay")
    exchange(1, "receive")

    @pl.when(parity == 1)
    def _():
        offset_copy.wait_recv()

    sources(1)

    @pl.when(parity == 0)
    def _():
        offset_copy.wait_send()

    exchange(0, "drain")
    exchange(1, "drain")
    for step in range(1, 8):
        steep_copy(step).wait_send()


def shards(spectrum, sea_mask, owner_list, owner_count, slopes, friction, wind_angle):
    blocks = spectrum.reshape(OWN, TALL, COLS)
    vmem = pl.BlockSpec(memory_space=pltpu.VMEM)
    dma = pltpu.SemaphoreType.DMA
    result = pl.pallas_call(
        kernel,
        out_shape=jax.ShapeDtypeStruct((OWN, TALL, COLS), jnp.float32),
        in_specs=[
            pl.BlockSpec(memory_space=pl.ANY),
            pl.BlockSpec(memory_space=pltpu.SMEM),
            vmem,
            vmem,
            vmem,
            vmem,
        ],
        out_specs=vmem,
        scratch_shapes=[
            pltpu.VMEM((OWN + 4, TALL, COLS), jnp.float32),
            pltpu.VMEM((OWN + 2 * REACH, TALL, COLS), jnp.float32),
            pltpu.VMEM((2, 5, PACK, COLS), jnp.float32),
            pltpu.VMEM((2, 5, PACK, COLS), jnp.float32),
            pltpu.VMEM((2, 5, ROWS, 128), jnp.float32),
            pltpu.VMEM((2, 5, ROWS, 128), jnp.float32),
            pltpu.VMEM((8, ROWS, COLS), jnp.float32),
            pltpu.VMEM((OWN + 1, ROWS, COLS), jnp.float32),
            dma,
            dma((2, 2)),
            dma((2, 2)),
            dma((2, 2)),
            dma((2, 2)),
            dma((2,)),
            dma((2,)),
            dma((OWN + 2 * REACH,)),
            dma((OWN + 2 * REACH,)),
            dma((OWN + 2 * REACH,)),
            dma((OWN + 2 * REACH,)),
            dma((OWN + 2 * REACH,)),
            dma((8,)),
            dma((8,)),
            dma,
            dma,
        ],
        compiler_params=pltpu.CompilerParams(
            collective_id=0, has_side_effects=True, vmem_limit_bytes=40 << 20
        ),
        name="wave_step",
    )(blocks, jnp.asarray(tables()), sea_mask, slopes, friction, wind_angle)
    return result.reshape(spectrum.shape)


def solution(mesh):
    in_specs = (
        P("comp", "tx", "ty"),
        P("tx", "ty"),
        P("tx", "ty", None, None),
        P("tx", "ty", None),
        P(None, "tx", "ty"),
        P("tx", "ty"),
        P("tx", "ty"),
    )
    out_specs = P("comp", "tx", "ty")
    return jax.shard_map(shards, mesh=mesh, in_specs=in_specs, out_specs=out_specs, check_vma=False)
```

profile of v0, /device:TPU:1, one launch (start us, length us, event | category | flops | bytes accessed | tf_op | source)
XLA Modules:
  0.0 71.6 jit_solution(6474712843556335327)
XLA Ops:
  0.0 0.0 copy-start
  0.0 1.5 %copy-done = f32[225,8,256]{2,1,0:T(8,128)S(1)} copy-done((f32[225,8,256]{2,1,0:T(8,128)S(1)}, f32[225,8,256]{2,1,0:T(8,128)}, u32[]{:S(2)}) %copy-start) | copy-done | bytes 1843224
  1.5 0.0 copy-start.1
  1.5 0.7 copy-done.1
  2.2 0.0 copy-start.2
  2.2 0.7 copy-done.2
  2.9 0.0 copy-start.3
  2.9 0.7 copy-done.3
  3.6 0.0 copy-start.4
  3.6 0.7 copy-done.4
  4.3 0.0 copy-start.5
  4.3 0.7 copy-done.5
  5.0 65.4 %wave_step.1 = f32[9,200,256]{2,1,0:T(8,128)S(1)} custom-call(f32[9,200,256]{2,1,0:T(8,128)S(1)} %bitcast.3, f32[272]{0:T(512)S(1)} %copy-done.5, s32[8,256]{1,0:T(8,128)S(1)} %copy-done.2, f32[2,8,256]{2,1,0:T(8,128)S(1)} %copy-done.1, f32[8,256]{1,0:T(8,128)S(1)} %copy-done.3, f32[8,256]{1,0:T(8,128)S(1)} %copy-done.4), custom_call_target="tpu_custom_call" | custom-call | tf_op jit(solution)/shard_map/wave_step/pallas_call | solution.py:464
  70.4 1.2 %copy.8 = f32[225,8,256]{2,1,0:T(8,128)} copy(f32[225,8,256]{2,1,0:T(8,128)S(1)} %bitcast.2) | data formatting | bytes 3686400
Async XLA Ops:
  0.0 1.5 %copy-start = (f32[225,8,256]{2,1,0:T(8,128)S(1)}, f32[225,8,256]{2,1,0:T(8,128)}, u32[]{:S(2)}) copy-start(f32[225,8,256]{2,1,0:T(8,128)} %param.8) | copy-start | bytes 5529604
  1.5 0.7 %copy-start.1 = (f32[2,8,256]{2,1,0:T(8,128)S(1)}, f32[2,8,256]{2,1,0:T(8,128)}, u32[]{:S(2)}) copy-start(f32[2,8,256]{2,1,0:T(8,128)} %slopes.1) | copy-start | bytes 49156
  2.2 0.7 copy-start.2
  2.9 0.7 copy-start.3
  3.6 0.7 copy-start.4
  4.3 0.7 copy-start.5
where the time goes:
time: 72 us; the launch traced here: 71.6 us
  Pallas kernels  65.4 us (91%)
  local copies, waits for them, and re-layouts  6.22 us (9%)
    pallas_call x1, Pallas kernels, shards(): pl.pallas_call(kernel, out_shape=jax.ShapeDtypeStruct((OWN, TALL, COLS),...  65.4 us
    unnamed x13, local copies, waits for them, and re-layouts  6.22 us

commit v1 on v0

v1 whole, which is shorter than its diff:
```python
import math

import jax
import jax.numpy as jnp
import numpy as np
from jax import lax
from jax.experimental import pallas as pl
from jax.experimental.pallas import tpu as pltpu
from jax.sharding import PartitionSpec as P

NDIR = 36
NFREQ = 50
HALF = 25
OWN = 9
REACH = 16
ROWS = 8
COLS = 256
TALL = HALF * ROWS
PHASES = ((0, 0, 5), (0, 5, 10), (0, 15, 10), (1, 0, 10), (1, 10, 10), (1, 20, 5))
EARLY = 3

TIME_STEP = 240.0
CELL_SIZE = 11100.0
GRAVITY = 9.81
LOW_FREQ = 0.0373
HIGH_FREQ = 1.0
WIND_GROWTH = 0.0001
WIND_FACTOR = 28.0
SATURATION_LOSS = 0.0005
CUMULATIVE_LOSS = 0.001
STEEPNESS_LOSS = 0.005
SATURATION_LEVEL = 0.6

T_COS, T_SIN, T_SPEED, T_BEND, T_OMEGA, T_STEEP, T_END = 0, 36, 72, 122, 172, 222, 272


def tables():
    heading = 2.0 * math.pi / NDIR * np.arange(NDIR)
    omega = 2.0 * math.pi * LOW_FREQ * (HIGH_FREQ / LOW_FREQ) ** (np.arange(NFREQ) / (NFREQ - 1))
    speed = TIME_STEP / CELL_SIZE * GRAVITY / (2.0 * omega)
    bend = TIME_STEP * NDIR / (2.0 * math.pi) * (2.0 * math.pi * LOW_FREQ) / omega
    steep = (omega / omega[-1]) ** 2 / (NDIR * NFREQ)
    return np.concatenate([np.cos(heading), np.sin(heading), speed, bend, omega, steep]).astype(
        np.float32
    )


def spread_weights():
    weights = np.cos(2.0 * math.pi / NDIR * np.arange(REACH // 2 + 1)) ** 2
    total = weights[0] + 2.0 * np.sum(weights[1:])
    return [float(w) for w in weights / total / SATURATION_LEVEL]


def lon_rows(phase):
    return (5 * PHASES[phase][2] + ROWS - 1) // ROWS * ROWS


def lon_base(phase):
    return sum(lon_rows(p) for p in range(phase))


def kernel(
    spec,
    table_in,
    sea_in,
    slopes_in,
    friction_in,
    wind_in,
    out,
    raw,
    moved,
    lon_out,
    lon_in,
    lat_out,
    lat_in,
    steep,
    offset,
    table,
    sea_mask,
    slopes,
    friction,
    wind,
    load_sem,
    raw_send,
    raw_recv,
    lon_send,
    lon_recv,
    lat_send,
    lat_recv,
    block_send,
    block_recv,
    steep_send,
    steep_recv,
    offset_send,
    offset_recv,
):
    comp = lax.axis_index("comp")
    tx = lax.axis_index("tx")
    ty = lax.axis_index("ty")
    parity = comp % 2
    quadrant = comp // 2
    pos_x = 1 - ((quadrant + 1) // 2) % 2
    pos_y = 1 - quadrant // 2

    def at_comp(step):
        return {"comp": (comp + step + 8) % 8}

    def remote(src, dst, send, recv, device):
        return pltpu.make_async_remote_copy(
            src_ref=src,
            dst_ref=dst,
            send_sem=send,
            recv_sem=recv,
            device_id=device,
            device_id_type=pl.DeviceIdType.MESH,
        )

    barrier = pltpu.get_barrier_semaphore()

    def greet(device):
        pl.semaphore_signal(barrier, inc=1, device_id=device, device_id_type=pl.DeviceIdType.MESH)

    for step in (4, 3, 5, 2, 6, 1, 7):
        greet(at_comp(step))
    for step in (1, -1):
        greet({"tx": (tx + step + 8) % 8})
        greet({"ty": (ty + step + 4) % 4})

    pairs = [
        (sea_in, sea_mask),
        (spec, raw.at[2 : 2 + OWN]),
        (table_in, table),
        (slopes_in, slopes),
        (friction_in, friction),
        (wind_in, wind),
    ]
    loads = [pltpu.make_async_copy(src, dst, load_sem.at[i]) for i, (src, dst) in enumerate(pairs)]
    for load in loads:
        load.start()

    row_ids = lax.broadcasted_iota(jnp.int32, (ROWS, COLS), 0)
    lane_ids = lax.broadcasted_iota(jnp.int32, (ROWS, 128), 1)
    inflow_row = row_ids == (1 - pos_x) * (ROWS - 1)
    last_lane_in = (1 - pos_y) * 127
    inflow_lane = lane_ids == last_lane_in
    up_y = jnp.zeros((ROWS, 128), jnp.int32) + pos_y > 0
    row_shift = jnp.where(pos_x > 0, 1, ROWS - 1)
    lane_shift = jnp.where(pos_y > 0, 1, 127)
    last_row = pos_x * (ROWS - 1)
    last_lane = pos_y * 127
    last_half = pl.multiple_of(pos_y * 128, 128)

    for load in loads:
        load.wait()
    sea = sea_mask[...].astype(jnp.float32)
    sea_row = jnp.sum(jnp.where(row_ids == last_row, sea, 0.0), axis=0, keepdims=True)
    sea_half = jnp.where(up_y, sea[:, 128:], sea[:, :128])

    def first_block(phase):
        return (PHASES[phase][0] + parity) % 2

    def span(phase):
        _, start, count = PHASES[phase]
        return pl.ds(ROWS * start, ROWS * count)

    def pack(phase):
        _, start, count = PHASES[phase]
        first = first_block(phase)

        def pack_block(t, carry):
            block = first + 2 * t

            def pack_one(i, lat):
                j = start + i
                lon_out[pl.ds(lon_base(phase) + count * t + i, 1), :] = (
                    raw[2 + block, pl.ds(ROWS * j + last_row, 1), :] * sea_row
                )
                rows = pl.ds(pl.multiple_of(ROWS * j, ROWS), ROWS)
                side = raw[2 + block, rows, pl.ds(last_half, 128)]
                turned = pltpu.roll(side * sea_half, (j - last_lane + 128) % 128, 1)
                return jnp.where(lane_ids == j, turned, lat)

            lat_out[phase, t] = lax.fori_loop(
                0, count, pack_one, jnp.zeros((ROWS, 128), jnp.float32), unroll=5
            )
            return carry

        lax.fori_loop(0, 5 - first, pack_block, 0)

    def raw_copies(phase):
        first = first_block(phase)
        rows = span(phase)
        return [
            remote(
                spec.at[first, rows],
                raw.at[11 + first, rows],
                raw_send,
                raw_recv.at[phase],
                at_comp(-1),
            ),
            remote(
                spec.at[8 - first, rows],
                raw.at[1 - first, rows],
                raw_send,
                raw_recv.at[phase],
                at_comp(1),
            ),
        ]

    lon_to = {"tx": (tx + 2 * pos_x - 1 + 8) % 8}
    lat_to = {"ty": (ty + 2 * pos_y - 1 + 4) % 4}

    def lon_copy(phase):
        rows = pl.ds(lon_base(phase), lon_rows(phase))
        return remote(lon_out.at[rows], lon_in.at[rows], lon_send, lon_recv.at[phase], lon_to)

    def lat_copy(phase):
        return remote(lat_out.at[phase], lat_in.at[phase], lat_send, lat_recv.at[phase], lat_to)

    def wait_halos(phase):
        both = raw.at[0:2, span(phase)]
        remote(both, both, raw_send, raw_recv.at[phase], at_comp(1)).wait_recv()
        lon_copy(phase).wait_recv()
        lat_copy(phase).wait_recv()

    lat_open = jnp.where(pos_y > 0, ty, 3 - ty) > 0
    lat_gate = jnp.where(lat_open, 1.0, 0.0)
    slope_x = slopes[0]
    slope_y = slopes[1]

    def advect(phase, steepness):
        _, start, count = PHASES[phase]
        first = first_block(phase)

        def one_block(t, steepness):
            block = first + 2 * t
            place = OWN * comp + block
            heading = place // 2
            freq = HALF * (place % 2)
            cos = table[T_COS + heading]
            sin = table[T_SIN + heading]
            abs_cos = jnp.abs(cos)
            abs_sin = jnp.abs(sin)
            bend_x = sin * slope_x - cos * slope_y
            lat = lat_in[phase, t] * lat_gate

            def one(i, steepness):
                j = start + i
                rows = pl.ds(pl.multiple_of(ROWS * j, ROWS), ROWS)
                centre = raw[2 + block, rows, :]
                prev_dir = raw[block, rows, :]
                next_dir = raw[4 + block, rows, :]
                masked = centre * sea
                up_lon = jnp.where(
                    inflow_row,
                    jnp.broadcast_to(lon_in[pl.ds(lon_base(phase) + count * t + i, 1), :], (ROWS, COLS)),
                    pltpu.roll(masked, row_shift, 0),
                )
                side = pltpu.roll(lat, (last_lane_in - j + 128) % 128, 1)
                low = pltpu.roll(masked[:, :128], lane_shift, 1)
                high = pltpu.roll(masked[:, 128:], lane_shift, 1)
                low_up = jnp.where(inflow_lane, jnp.where(up_y, side, high), low)
                high_up = jnp.where(inflow_lane, jnp.where(up_y, low, side), high)
                up_lat = jnp.concatenate([low_up, high_up], axis=1)
                speed = table[T_SPEED + freq + j]
                turning = table[T_BEND + freq + j] * bend_x
                value = sea * (
                    centre
                    - (speed * abs_cos) * (centre - up_lon)
                    - (speed * abs_sin) * (centre - up_lat)
                    - (
                        jnp.maximum(turning, 0.0) * (centre - prev_dir)
                        + jnp.minimum(turning, 0.0) * (next_dir - centre)
                    )
                )
                moved[REACH // 2 + t, first, rows, :] = value
                return steepness + table[T_STEEP + freq + j] * value

            return lax.fori_loop(0, count, one, steepness, unroll=5)

        return lax.fori_loop(0, 5 - first, one_block, steepness)

    def shifted(side, phase, action):
        rows = span(phase)
        first = (PHASES[phase][0] + side) % 2
        mine, theirs = 5 - first, 4 + first
        partner, other = (1, -1) if side == 0 else (-1, 1)

        def block_copy(start, count, step, recv):
            place = REACH + first + 2 * start - OWN * step
            return remote(
                moved.at[REACH // 2 + start : REACH // 2 + start + count, first, rows],
                moved.at[place // 2 : place // 2 + count, place % 2, rows],
                block_send,
                block_recv.at[phase, recv],
                at_comp(step),
            )

        def relay():
            start = 1 - side
            place = REACH + 1 - first + 2 * start + OWN * other
            there = place - OWN * partner
            count = theirs - 1
            return remote(
                moved.at[place // 2 : place // 2 + count, place % 2, rows],
                moved.at[there // 2 : there // 2 + count, there % 2, rows],
                block_send,
                block_recv.at[phase, 1],
                at_comp(partner),
            )

        def arrived(count, recv):
            blocks = moved.at[0:count, 0, rows]
            remote(blocks, blocks, block_send, block_recv.at[phase, recv], at_comp(1)).wait_recv()

        if action == "send":
            block_copy(side, mine - 1, other, 0).start()
            block_copy(1 - side, mine - 1, 2 * partner, 1).start()
            block_copy(0 if side else mine - 1, 1, other, 1).start()
            block_copy(0, mine, partner, 1).start()
        elif action == "relay":
            arrived(theirs - 1, 0)
            relay().start()
        else:
            arrived(theirs + 1 + 2 * (mine - 1), 1)

    def exchange(phase, action):
        for side in (0, 1):

            @pl.when(parity == side)
            def _():
                shifted(side, phase, action)

    def steep_copy(step):
        return remote(
            steep.at[comp], steep.at[comp], steep_send, steep_recv, at_comp(step)
        )

    pack(0)
    pl.semaphore_wait(barrier, 11)
    for phase in range(len(PHASES)):
        for copy in raw_copies(phase):
            copy.start()
    for phase in range(len(PHASES)):
        if phase:
            pack(phase)
        lon_copy(phase).start()
        lat_copy(phase).start()

    partial = jnp.zeros((ROWS, COLS), jnp.float32)
    for phase in range(len(PHASES)):
        wait_halos(phase)
        partial = advect(phase, partial)
        if phase < EARLY:
            exchange(phase, "send")
    steep[comp] = partial
    for step in range(1, 8):
        steep_copy(step).start()
    for phase in range(EARLY, len(PHASES)):
        exchange(phase, "send")

    weights = spread_weights()
    wind_x = (WIND_FACTOR / GRAVITY) * friction[...] * jnp.cos(wind[...])
    wind_y = (WIND_FACTOR / GRAVITY) * friction[...] * jnp.sin(wind[...])
    at_sea = sea > 0.5

    exchange(0, "relay")
    seven = steep.at[0:7]
    remote(seven, seven, steep_send, steep_recv, at_comp(1)).wait_recv()
    total = steep[0]
    for slot in range(1, 8):
        total = total + steep[slot]
    steep_loss = (TIME_STEP * STEEPNESS_LOSS) * total * total

    def sources(phase):
        upper, start, count = PHASES[phase]
        first = first_block(phase)

        def one_block(t, carry):
            block = first + 2 * t
            place = OWN * comp + block
            heading = place // 2
            freq = HALF * (place % 2)
            cos = table[T_COS + heading]
            sin = table[T_SIN + heading]
            along = cos * wind_x + sin * wind_y

            def one(i, running):
                j = start + i
                rows = pl.ds(pl.multiple_of(ROWS * j, ROWS), ROWS)
                centre = moved[REACH // 2 + t, first, rows, :]
                level = weights[0] * centre
                for m in range(1, REACH // 2 + 1):
                    level = level + weights[m] * (
                        moved[REACH // 2 + t - m, first, rows, :]
                        + moved[REACH // 2 + t + m, first, rows, :]
                    )
                excess = jnp.maximum(level - 1.0, 0.0)
                excess_sq = excess * excess
                omega = table[T_OMEGA + freq + j]
                growth = (TIME_STEP * WIND_GROWTH * omega) * jnp.maximum(omega * along - 1.0, 0.0)
                losses = omega * (
                    (TIME_STEP * SATURATION_LOSS) * excess_sq
                    + (TIME_STEP * CUMULATIVE_LOSS / NFREQ) * running
                    + steep_loss
                )
                updated = centre * (1.0 + growth) / (1.0 + losses)
                out[block, rows, :] = jnp.where(at_sea, updated, centre)
                return running + excess_sq

            if start > 0:
                before = offset[block + 1]
            elif upper:
                before = offset[block]
            else:
                before = jnp.zeros((ROWS, COLS), jnp.float32)
            offset[block + 1] = lax.fori_loop(0, count, one, before, unroll=5)
            return carry

        lax.fori_loop(0, 5 - first, one_block, 0)

    offset_copy = remote(
        offset.at[OWN], offset.at[0], offset_send, offset_recv, {"comp": comp + 1 - 2 * parity}
    )
    for phase, (upper, start, count) in enumerate(PHASES):
        if phase:
            exchange(phase, "relay")
        exchange(phase, "receive")
        if upper and start == 0:

            @pl.when(parity == 1)
            def _():
                offset_copy.wait_recv()

        sources(phase)
        if not upper and start + count == HALF:

            @pl.when(parity == 0)
            def _():
                offset_copy.start()

    @pl.when(parity == 0)
    def _():
        offset_copy.wait_send()

    for sent, sem in (
        (raw.at[0:4], raw_send),
        (lon_out, lon_send),
        (lat_out, lat_send),
        (moved.at[0:16], block_send),
        (seven, steep_send),
    ):
        remote(sent, sent, sem, raw_recv.at[0], at_comp(1)).wait_send()


def shards(spectrum, sea_mask, owner_list, owner_count, slopes, friction, wind_angle):
    blocks = spectrum.reshape(OWN, TALL, COLS)
    hbm = pl.BlockSpec(memory_space=pltpu.HBM)
    dma = pltpu.SemaphoreType.DMA
    phases = len(PHASES)
    operands = [blocks, jnp.asarray(tables()), sea_mask, slopes, friction, wind_angle]
    result = pl.pallas_call(
        kernel,
        out_shape=jax.ShapeDtypeStruct((OWN, TALL, COLS), jnp.float32),
        in_specs=[hbm] * 6,
        out_specs=pl.BlockSpec(memory_space=pltpu.VMEM),
        scratch_shapes=[
            pltpu.VMEM((OWN + 4, TALL, COLS), jnp.float32),
            pltpu.VMEM((OWN // 2 + 1 + REACH, 2, TALL, COLS), jnp.float32),
            pltpu.VMEM((lon_base(phases), COLS), jnp.float32),
            pltpu.VMEM((lon_base(phases), COLS), jnp.float32),
            pltpu.VMEM((phases, 5, ROWS, 128), jnp.float32),
            pltpu.VMEM((phases, 5, ROWS, 128), jnp.float32),
            pltpu.VMEM((8, ROWS, COLS), jnp.float32),
            pltpu.VMEM((OWN + 1, ROWS, COLS), jnp.float32),
            pltpu.SMEM((T_END,), jnp.float32),
            pltpu.VMEM((ROWS, COLS), jnp.int32),
            pltpu.VMEM((2, ROWS, COLS), jnp.float32),
            pltpu.VMEM((ROWS, COLS), jnp.float32),
            pltpu.VMEM((ROWS, COLS), jnp.float32),
            dma((6,)),
            dma,
            dma((phases,)),
            dma,
            dma((phases,)),
            dma,
            dma((phases,)),
            dma,
            dma((phases, 2)),
            dma,
            dma,
            dma,
            dma,
        ],
        compiler_params=pltpu.CompilerParams(
            collective_id=0, has_side_effects=True, vmem_limit_bytes=40 << 20
        ),
        name="wave_step",
    )(*[pltpu.with_memory_space_constraint(x, pltpu.HBM) for x in operands])
    return result.reshape(spectrum.shape)


def solution(mesh):
    in_specs = (
        P("comp", "tx", "ty"),
        P("tx", "ty"),
        P("tx", "ty", None, None),
        P("tx", "ty", None),
        P(None, "tx", "ty"),
        P("tx", "ty"),
        P("tx", "ty"),
    )
    out_specs = P("comp", "tx", "ty")
    return jax.shard_map(shards, mesh=mesh, in_specs=in_specs, out_specs=out_specs, check_vma=False)
```

time: 72 us -> 53.9 us (0.75)
  Pallas kernels: 65.4 us -> 52.6 us
  local copies, waits for them, and re-layouts: 6.22 us -> 1.23 us
    pallas_call x1, Pallas kernels: 65.4 us -> 52.6 us  [shards(): pl.pallas_call(kernel, out_shape=jax.ShapeDtypeStruct((OWN, TALL, COLS),...]
    unnamed x13 -> x1, local copies, waits for them, and re-layouts: 6.22 us -> 1.23 us
where the time goes in v1:
time: 53.9 us; the launch traced here: 53.8 us
  Pallas kernels  52.6 us (98%)
  local copies, waits for them, and re-layouts  1.23 us (2%)
    pallas_call x1, Pallas kernels, shards(): pl.pallas_call(kernel, out_shape=jax.ShapeDtypeStruct((OWN, TALL, COLS),...  52.6 us
    unnamed x1, local copies, waits for them, and re-layouts  1.23 us

profile of v1, /device:TPU:1, one launch (start us, length us, event | category | flops | bytes accessed | tf_op | source)
XLA Modules:
  0.0 53.8 jit_solution(17893228225289106589)
XLA Ops:
  0.0 52.6 %wave_step.1 = f32[9,200,256]{2,1,0:T(8,128)S(1)} custom-call(f32[9,200,256]{2,1,0:T(8,128)} %bitcast.3, f32[272]{0:T(512)} %constant.2.clone.table_in, s32[8,256]{1,0:T(8,128)} %sea_in.1, f32[2,8,256]{2,1,0:T(8,128)} %slopes_in.1, f32[8,256]{1,0:T(8,128)} %friction_in.1, f32[8,256]{1,0:T(8,128)} %wind_in.1), custom_call_target="tpu_custom_call" | custom-call | tf_op jit(solution)/shard_map/wave_step/pallas_call | solution.py:462
  52.6 1.2 %copy.8 = f32[225,8,256]{2,1,0:T(8,128)} copy(f32[225,8,256]{2,1,0:T(8,128)S(1)} %bitcast.2) | data formatting | bytes 3686400

commit v2 on v1

--- a/solution.py
+++ b/solution.py
@@ -120,7 +120,7 @@
     def greet(device):
         pl.semaphore_signal(barrier, inc=1, device_id=device, device_id_type=pl.DeviceIdType.MESH)
 
-    for step in (4, 3, 5, 2, 6, 1, 7):
+    for step in (4, 2, 6, 1, 7):
         greet(at_comp(step))
     for step in (1, -1):
         greet({"tx": (tx + step + 8) % 8})
@@ -128,7 +128,8 @@
 
     pairs = [
         (sea_in, sea_mask),
-        (spec, raw.at[2 : 2 + OWN]),
+        (spec.at[:, 0:40], raw.at[2 : 2 + OWN, 0:40]),
+        (spec.at[:, 40:], raw.at[2 : 2 + OWN, 40:]),
         (table_in, table),
         (slopes_in, slopes),
         (friction_in, friction),
@@ -150,42 +151,12 @@
     last_lane = pos_y * 127
     last_half = pl.multiple_of(pos_y * 128, 128)
 
-    for load in loads:
-        load.wait()
-    sea = sea_mask[...].astype(jnp.float32)
-    sea_row = jnp.sum(jnp.where(row_ids == last_row, sea, 0.0), axis=0, keepdims=True)
-    sea_half = jnp.where(up_y, sea[:, 128:], sea[:, :128])
-
     def first_block(phase):
         return (PHASES[phase][0] + parity) % 2
 
     def span(phase):
         _, start, count = PHASES[phase]
         return pl.ds(ROWS * start, ROWS * count)
-
-    def pack(phase):
-        _, start, count = PHASES[phase]
-        first = first_block(phase)
-
-        def pack_block(t, carry):
-            block = first + 2 * t
-
-            def pack_one(i, lat):
-                j = start + i
-                lon_out[pl.ds(lon_base(phase) + count * t + i, 1), :] = (
-                    raw[2 + block, pl.ds(ROWS * j + last_row, 1), :] * sea_row
-                )
-                rows = pl.ds(pl.multiple_of(ROWS * j, ROWS), ROWS)
-                side = raw[2 + block, rows, pl.ds(last_half, 128)]
-                turned = pltpu.roll(side * sea_half, (j - last_lane + 128) % 128, 1)
-                return jnp.where(lane_ids == j, turned, lat)
-
-            lat_out[phase, t] = lax.fori_loop(
-                0, count, pack_one, jnp.zeros((ROWS, 128), jnp.float32), unroll=5
-            )
-            return carry
-
-        lax.fori_loop(0, 5 - first, pack_block, 0)
 
     def raw_copies(phase):
         first = first_block(phase)
@@ -206,6 +177,40 @@
                 at_comp(1),
             ),
         ]
+    pl.semaphore_wait(barrier, 9)
+    for phase in range(len(PHASES)):
+        for copy in raw_copies(phase):
+            copy.start()
+    for i, load in enumerate(loads):
+        if i != 2:
+            load.wait()
+    sea = sea_mask[...].astype(jnp.float32)
+    sea_row = jnp.sum(jnp.where(row_ids == last_row, sea, 0.0), axis=0, keepdims=True)
+    sea_half = jnp.where(up_y, sea[:, 128:], sea[:, :128])
+
+    def pack(phase):
+        _, start, count = PHASES[phase]
+        first = first_block(phase)
+
+        def pack_block(t, carry):
+            block = first + 2 * t
+
+            def pack_one(i, lat):
+                j = start + i
+                lon_out[pl.ds(lon_base(phase) + count * t + i, 1), :] = (
+                    raw[2 + block, pl.ds(ROWS * j + last_row, 1), :] * sea_row
+                )
+                rows = pl.ds(pl.multiple_of(ROWS * j, ROWS), ROWS)
+                side = raw[2 + block, rows, pl.ds(last_half, 128)]
+                turned = pltpu.roll(side * sea_half, (j - last_lane + 128) % 128, 1)
+                return jnp.where(lane_ids == j, turned, lat)
+
+            lat_out[phase, t] = lax.fori_loop(
+                0, count, pack_one, jnp.zeros((ROWS, 128), jnp.float32), unroll=5
+            )
+            return carry
+
+        lax.fori_loop(0, 5 - first, pack_block, 0)
 
     lon_to = {"tx": (tx + 2 * pos_x - 1 + 8) % 8}
     lat_to = {"ty": (ty + 2 * pos_y - 1 + 4) % 4}
@@ -331,21 +336,21 @@
             def _():
                 shifted(side, phase, action)
 
-    def steep_copy(step):
-        return remote(
-            steep.at[comp], steep.at[comp], steep_send, steep_recv, at_comp(step)
-        )
-
-    pack(0)
-    pl.semaphore_wait(barrier, 11)
-    for phase in range(len(PHASES)):
-        for copy in raw_copies(phase):
-            copy.start()
-    for phase in range(len(PHASES)):
-        if phase:
-            pack(phase)
+    def steep_copy(src, dst, stage, step):
+        return remote(steep.at[src], steep.at[dst], steep_send, steep_recv.at[stage], at_comp(step))
+
+    def steep_wait(first, count, stage):
+        blocks = steep.at[first : first + count]
+        remote(blocks, blocks, steep_send, steep_recv.at[stage], at_comp(1)).wait_recv()
+
+    def give(phase):
+        pack(phase)
         lon_copy(phase).start()
         lat_copy(phase).start()
+
+    give(0)
+    loads[2].wait()
+    give(1)
 
     partial = jnp.zeros((ROWS, COLS), jnp.float32)
     for phase in range(len(PHASES)):
@@ -353,9 +358,21 @@
         partial = advect(phase, partial)
         if phase < EARLY:
             exchange(phase, "send")
-    steep[comp] = partial
-    for step in range(1, 8):
-        steep_copy(step).start()
+        if phase + 2 < len(PHASES):
+            give(phase + 2)
+    steep[0] = partial
+
+    @pl.when(parity == 1)
+    def _():
+        steep_copy(0, 1, 0, -1).start()
+
+    @pl.when(parity == 0)
+    def _():
+        steep_wait(1, 1, 0)
+        steep[2] = steep[0] + steep[1]
+        for i in range(3):
+            steep_copy(2, 3 + i, 1, 2 * i + 2).start()
+
     for phase in range(EARLY, len(PHASES)):
         exchange(phase, "send")
 
@@ -365,11 +382,18 @@
     at_sea = sea > 0.5
 
     exchange(0, "relay")
-    seven = steep.at[0:7]
-    remote(seven, seven, steep_send, steep_recv, at_comp(1)).wait_recv()
-    total = steep[0]
-    for slot in range(1, 8):
-        total = total + steep[slot]
+
+    @pl.when(parity == 0)
+    def _():
+        steep_wait(3, 3, 1)
+        steep[6] = (steep[2] + steep[4]) + (steep[3] + steep[5])
+        steep_copy(6, 6, 2, 1).start()
+
+    @pl.when(parity == 1)
+    def _():
+        steep_wait(6, 1, 2)
+
+    total = steep[6]
     steep_loss = (TIME_STEP * STEEPNESS_LOSS) * total * total
 
     def sources(phase):
@@ -448,9 +472,14 @@
         (lon_out, lon_send),
         (lat_out, lat_send),
         (moved.at[0:16], block_send),
-        (seven, steep_send),
     ):
         remote(sent, sent, sem, raw_recv.at[0], at_comp(1)).wait_send()
+    for side, count in ((0, 4), (1, 1)):
+
+        @pl.when(parity == side)
+        def _():
+            sums = steep.at[0:count]
+            remote(sums, sums, steep_send, raw_recv.at[0], at_comp(1)).wait_send()
 
 
 def shards(spectrum, sea_mask, owner_list, owner_count, slopes, friction, wind_angle):
@@ -478,7 +507,7 @@
             pltpu.VMEM((2, ROWS, COLS), jnp.float32),
             pltpu.VMEM((ROWS, COLS), jnp.float32),
             pltpu.VMEM((ROWS, COLS), jnp.float32),
-            dma((6,)),
+            dma((7,)),
             dma,
             dma((phases,)),
             dma,
@@ -488,7 +517,7 @@
             dma,
             dma((phases, 2)),
             dma,
-            dma,
+            dma((3,)),
             dma,
             dma,
         ],

time: 53.9 us -> 53.7 us (level)
  no operation moved by 1% of the time
where the time goes in v2:
time: 53.7 us; the launch traced here: 53.6 us
  Pallas kernels  52.4 us (98%)
  local copies, waits for them, and re-layouts  1.23 us (2%)
    pallas_call x1, Pallas kernels, shards(): pl.pallas_call(kernel, out_shape=jax.ShapeDtypeStruct((OWN, TALL, COLS),...  52.4 us
    unnamed x1, local copies, waits for them, and re-layouts  1.23 us

profile of v2, /device:TPU:1, one launch (start us, length us, event | category | flops | bytes accessed | tf_op | source)
XLA Modules:
  0.0 53.6 jit_solution(5293588312276617867)
XLA Ops:
  0.0 52.4 %wave_step.1 = f32[9,200,256]{2,1,0:T(8,128)S(1)} custom-call(f32[9,200,256]{2,1,0:T(8,128)} %bitcast.3, f32[272]{0:T(512)} %constant.2.clone.table_in, s32[8,256]{1,0:T(8,128)} %sea_in.1, f32[2,8,256]{2,1,0:T(8,128)} %slopes_in.1, f32[8,256]{1,0:T(8,128)} %friction_in.1, f32[8,256]{1,0:T(8,128)} %wind_in.1), custom_call_target="tpu_custom_call" | custom-call | tf_op jit(solution)/shard_map/wave_step/pallas_call | solution.py:491
  52.4 1.2 %copy.8 = f32[225,8,256]{2,1,0:T(8,128)} copy(f32[225,8,256]{2,1,0:T(8,128)S(1)} %bitcast.2) | data formatting | bytes 3686400

commit v3 on v2

--- a/solution.py
+++ b/solution.py
@@ -438,7 +438,7 @@
                 before = offset[block]
             else:
                 before = jnp.zeros((ROWS, COLS), jnp.float32)
-            offset[block + 1] = lax.fori_loop(0, count, one, before, unroll=5)
+            offset[block + 1] = lax.fori_loop(0, count, one, before, unroll=count)
             return carry
 
         lax.fori_loop(0, 5 - first, one_block, 0)

time: 53.7 us -> 53.7 us (level)
  no operation moved by 1% of the time
where the time goes in v3:
time: 53.7 us; the launch traced here: 53.6 us
  Pallas kernels  52.4 us (98%)
  local copies, waits for them, and re-layouts  1.23 us (2%)
    pallas_call x1, Pallas kernels, shards(): pl.pallas_call(kernel, out_shape=jax.ShapeDtypeStruct((OWN, TALL, COLS),...  52.4 us
    unnamed x1, local copies, waits for them, and re-layouts  1.23 us

profile of v3, /device:TPU:1, one launch (start us, length us, event | category | flops | bytes accessed | tf_op | source)
XLA Modules:
  0.0 53.6 jit_solution(4685471459069198140)
XLA Ops:
  0.0 52.4 %wave_step.1 = f32[9,200,256]{2,1,0:T(8,128)S(1)} custom-call(f32[9,200,256]{2,1,0:T(8,128)} %bitcast.3, f32[272]{0:T(512)} %constant.2.clone.table_in, s32[8,256]{1,0:T(8,128)} %sea_in.1, f32[2,8,256]{2,1,0:T(8,128)} %slopes_in.1, f32[8,256]{1,0:T(8,128)} %friction_in.1, f32[8,256]{1,0:T(8,128)} %wind_in.1), custom_call_target="tpu_custom_call" | custom-call | tf_op jit(solution)/shard_map/wave_step/pallas_call | solution.py:491
  52.4 1.2 %copy.8 = f32[225,8,256]{2,1,0:T(8,128)} copy(f32[225,8,256]{2,1,0:T(8,128)S(1)} %bitcast.2) | data formatting | bytes 3686400
